TPU v7x, 32 devices: a whole 2x2x4 slice. The times are simulated.
32 devices in a mesh: grp: 4 (over x, core), dev: 8 (over z, y).
Axes of the slice: x: 2, y: 2, z: 4, core: 2. Of those that a mesh axis runs over, the one named last changes fastest.
Arguments:
- positions: float32 [3, 32768], P(None, ('grp', 'dev')), may hold values from -6 to 6
- rotations: float32 [9, 32768], P(None, ('grp', 'dev')), may hold values from -1 to 1, as said below
- clump_kind: int32 [32768], P(('grp', 'dev')), may hold values from 0 to 7
- sub_offsets: int32 [8, 3, 64], replicated, may hold values from -8 to 8
- pair_blocks: int32 [2, 32768], P(None, ('grp', 'dev')), may hold values from 0 to 16383, as said below
- pair_count: int32 [32], P(('grp', 'dev')), may hold values from 1 to 1024, as said below
Outputs:
- clump_force: float32 [3, 32768], P(None, ('grp', 'dev'))
- clump_torque: float32 [3, 32768], P(None, ('grp', 'dev'))
Inputs may be any that keep to these rules, and one draw needn't show every extreme that they name: `rotations`: each column is a proper rotation matrix in row-major order. `pair_blocks`: the two blocks of a slot differ. A slot on a device of group g names as its first block one of group g's blocks (g * 4096 to (g + 1) * 4096 - 1) and as its second one of group g's blocks or of the 128 nearest blocks of groups g - 1 and g + 1, that is a block from g * 4096 - 128 to (g + 1) * 4096 + 127. `pair_count`: each device has at least one live slot.
All inputs are finite; a program needn't handle non-finite values.
Results may differ from a plain program's by a relative error of at most 0.0003.
Values sent between devices are 32-bit elements; how exact they have to be, the bound alone decides.
No kernel may reach another device: no remote copies, remote signals or barrier semaphores. Data moves between devices by JAX's collectives and lax.ppermute only.
A program may use at most 128 MiB of HBM per device.

v0:
```python
import jax
import jax.numpy as jnp
from jax import lax
from jax.sharding import PartitionSpec as P

RIM = 128
OFFSET_UNIT = 0.125
REACH_SQUARED = 4.0
STIFFNESS = 1.0 / 256.0


def padded(cells, sides, width):
    for axis, dim in sides:
        count = lax.axis_size(axis)
        ends = count - 1
        head = lax.slice_in_dim(cells, 0, width, axis=dim)
        tail = lax.slice_in_dim(cells, cells.shape[dim] - width, cells.shape[dim], axis=dim)
        cells = jnp.concatenate(
            [
                lax.ppermute(tail, axis, [(i, (i + 1) % count) for i in range(ends)]),
                cells,
                lax.ppermute(head, axis, [((i + 1) % count, i) for i in range(ends)]),
            ],
            axis=dim,
        )
    return cells


def cross_axis(left_vec, right_vec):
    return jnp.stack(
        [
            left_vec[1] * right_vec[2] - left_vec[2] * right_vec[1],
            left_vec[2] * right_vec[0] - left_vec[0] * right_vec[2],
            left_vec[0] * right_vec[1] - left_vec[1] * right_vec[0],
        ],
        0,
    )


def place_blocks(centers, rotation_rows, onehot, offset_table):
    sub_count = offset_table.shape[1] // 3
    offsets = jnp.dot(onehot, offset_table, precision=lax.Precision.HIGHEST).reshape(
        -1, 3, sub_count
    )
    rotation_mats = rotation_rows.T.reshape(-1, 3, 3)
    world_pos = centers.T[:, :, None] + jnp.einsum(
        "ckm,cms->cks", rotation_mats, offsets, precision=lax.Precision.HIGHEST
    )
    block_count = world_pos.shape[0] // 2
    return (
        world_pos.reshape(block_count, 2, 3, sub_count)
        .transpose(0, 2, 1, 3)
        .reshape(block_count, 3, 2 * sub_count)
    )


def contact(near_pos, far_pos):
    separation = near_pos[:, :, None] - far_pos[:, None, :]
    squared = jnp.sum(separation * separation, 0)
    weights = STIFFNESS * jnp.maximum(REACH_SQUARED - squared, 0.0)
    pushes = weights[None] * separation
    return (jnp.sum(pushes, 2), -jnp.sum(pushes, 1))


def anchor_moments(sphere_block, force_block):
    sub_count = sphere_block.shape[1] // 2
    spots = sphere_block.reshape(3, 2, sub_count)
    pushes = force_block.reshape(3, 2, sub_count)
    return jnp.concatenate([jnp.sum(pushes, -1), jnp.sum(cross_axis(spots, pushes), -1)], 0)


def shards(positions, rotations, clump_kind, sub_offsets, pair_blocks, pair_count):
    members = lax.axis_size("dev")
    group_index = lax.axis_index("grp")
    own_blocks = positions.shape[1] // 2
    group_blocks = own_blocks * members
    kind_count = sub_offsets.shape[0]
    sub_count = sub_offsets.shape[2]
    slot_group = 32
    offset_table = sub_offsets.astype(jnp.float32).reshape(kind_count, 3 * sub_count) * OFFSET_UNIT
    onehot = (clump_kind[:, None] == jnp.arange(kind_count, dtype=jnp.int32)[None, :]).astype(
        jnp.float32
    )
    own_spheres = place_blocks(positions, rotations, onehot, offset_table)
    gathered = lax.all_gather(own_spheres, "dev", axis=0, tiled=True)
    spheres = padded(gathered, (("grp", 0),), RIM)
    table_base = group_index * group_blocks - RIM
    first_local = pair_blocks[0] - table_base
    second_local = pair_blocks[1] - table_base
    live_count = pair_count[0]
    turn_count = (live_count + slot_group - 1) // slot_group
    table_rows = spheres.shape[0]
    zero_table = jnp.zeros((table_rows, 6, 2), jnp.float32)

    def visit_block(turn_index, totals):
        start_row = turn_index * slot_group
        first_block = lax.dynamic_slice_in_dim(first_local, start_row, slot_group, 0)
        second_block = lax.dynamic_slice_in_dim(second_local, start_row, slot_group, 0)
        live_part = (start_row + jnp.arange(slot_group, dtype=jnp.int32) < live_count).astype(
            jnp.float32
        )
        near_pos = spheres[first_block]
        far_pos = spheres[second_block]
        push_first, push_second = jax.vmap(contact)(near_pos, far_pos)
        weight_live = live_part[:, None, None]
        totals = totals.at[first_block].add(
            jax.vmap(anchor_moments)(near_pos, push_first) * weight_live
        )
        totals = totals.at[second_block].add(
            jax.vmap(anchor_moments)(far_pos, push_second) * weight_live
        )
        return totals

    totals = lax.fori_loop(0, turn_count, visit_block, zero_table)
    moments = totals.transpose(1, 0, 2).reshape(6, 2 * table_rows)
    rim_clumps = 2 * RIM
    rim_parts = jnp.concatenate(
        [moments[:, :rim_clumps], moments[:, moments.shape[1] - rim_clumps :]], 1
    )
    arrived = padded(rim_parts, (("grp", 1),), rim_clumps)
    interior = moments[:, rim_clumps : rim_clumps + 2 * group_blocks]
    interior = interior.at[:, :rim_clumps].add(arrived[:, :rim_clumps])
    interior = interior.at[:, interior.shape[1] - rim_clumps :].add(
        arrived[:, arrived.shape[1] - rim_clumps :]
    )
    summed = lax.psum_scatter(interior, "dev", scatter_dimension=1, tiled=True)
    clump_force = summed[0:3]
    clump_torque = summed[3:6] - cross_axis(positions, clump_force)
    return (clump_force, clump_torque)


def solution(mesh):
    placed = (
        P(None, ("grp", "dev")),
        P(None, ("grp", "dev")),
        P(("grp", "dev")),
        P(),
        P(None, ("grp", "dev")),
        P(("grp", "dev")),
    )
    return jax.shard_map(
        shards,
        mesh=mesh,
        in_specs=placed,
        out_specs=(P(None, ("grp", "dev")), P(None, ("grp", "dev"))),
        check_vma=False,
    )
```

profile of v0, /device:TPU:0, one launch (start us, length us, event | category | flops | bytes accessed | tf_op | source)
XLA Modules:
  0.0 1036.5 jit_solution(15804710355770445196)
XLA Ops:
  13.1 9.8 convolution_add_fusion
  26.1 100.9 %all-gather.2.cloned.1.call-done = f32[4096,3,128]{0,2,1:T(8,128)} async-done(((f32[512,3,128]{0,2,1:T(8,128)}), f32[4096,3,128]{0,2,1:T(8,128)}) %all-gather.2.cloned.1.call-update) | async-done | bytes 6291472 | tf_op jit(solution)/shard_map/all_gather | solution.py:85
  134.4 6.1 pad_maximum_fusion
  140.5 10.1 copy.151
  154.3 792.6 %while.12 = (s32[]{:T(128)}, f32[4352,6,2]{1,2,0:T(2,128)}, s32[]{:T(128)}, s32[1024]{0:T(1024)S(1)}, f32[4352,3,128]{2,1,0:T(4,128)}, /*index=5*/s32[1024]{0:T(...) while((s32[]{:T(128)}, f32[4352,6,2]{1,2,0:T(2,128)}, ...), condition=%wide.region_10.11_spmd, body=%wide.region_0.10_spmd.sunk | while | flops 12222438 | bytes 10249395 | solution.py:114
  154.3 4.1 gather_fusion
  179.1 4.1 gather_fusion
  183.3 4.1 gather_fusion.1
  257.4 4.1 gather_fusion.1
  278.1 4.1 gather_fusion
  307.1 4.1 gather_fusion.1
  331.9 4.1 gather_fusion.1
  356.7 4.1 gather_fusion.1
  402.0 4.1 gather_fusion
  406.2 4.1 gather_fusion.1
  455.8 4.1 gather_fusion.1
  480.4 4.1 gather_fusion.1
  579.5 4.1 gather_fusion.1
  628.9 4.1 gather_fusion.1
  703.3 4.1 gather_fusion.1
  847.8 4.1 gather_fusion
  852.0 4.1 gather_fusion.1
  949.9 4.4 slice.176
  961.1 66.2 %reduce-scatter.2.cloned.1.call-done = f32[6,1024]{1,0:T(8,128)} async-done(((f32[6,8192]{1,0:T(8,128)}), f32[6,1024]{1,0:T(8,128)}) %reduce-scatter.2.cloned.1.call-update) | async-done | bytes 24592 | tf_op jit(solution)/shard_map/reduce_scatter | solution.py:126
  (1080 shorter events, 748.9 us)
Async XLA Ops:
  7.2 5.7 copy-start.1
  7.2 119.8 %all-gather.2.cloned.1.call-start = ((), (), s32[]{:S(2)}) async-start(), calls=%async_computation.1 | async-start | bytes 7077888 | tf_op jit(solution)/shard_map/all_gather | solution.py:85
  13.1 117.6 %copy-start.2 = (s32[2,1024]{1,0:T(2,128)S(1)}, s32[2,1024]{1,0:T(2,128)}, u32[]{:S(2)}) copy-start(s32[2,1024]{1,0:T(2,128)} %param.16) | copy-start | bytes 24580
  25.4 1001.9 %reduce-scatter.2.cloned.1.call-start = ((), (), s32[]{:S(2)}) async-start(), calls=%async_computation.2 | async-start | bytes 294912 | tf_op jit(solution)/shard_map/reduce_scatter | solution.py:126
  128.0 2.6 collective-permute-start
  129.4 5.0 collective-permute-start.1
  948.0 10.6 %collective-permute-start.2 = (f32[6,256]{1,0:T(8,128)S(1)}, f32[6,256]{1,0:T(8,128)S(1)}, u32[]{:S(2)}, u32[]{:S(2)}) collective-permute-start(f32[6,256]{1,0:T(8,128)S(1)} %copy.158), channel_id=1, source_target_pairs={{0,8},{8,16},{16,24},{1,9},{9,17},{17,25},{2,10},{10,18},{18,26},{... | collective-permute-start | bytes 18440 | tf_op jit(solution)/shard_map/ppermute | solution.py:20
  957.3 3.1 collective-permute-start.3
  960.4 0.7 copy-start
Sparse Core Ops, SparseCore 0:
  25.5 101.4 all-gather.1
  961.2 66.0 reduce-scatter.1
where the time goes:
time: 1040 us
  other arithmetic  501 us (48%)
  local copies, waits for them, and re-layouts  328 us (32%)
  waiting for transfers between devices  172 us (17%)
  between operations  14.8 us (1%)
  matrix products  11 us (1%)
    gather x64, local copies, waits for them, and re-layouts, visit_block(): near_pos = spheres[first_block]  133 us
    gather x64, local copies, waits for them, and re-layouts, visit_block(): far_pos = spheres[second_block]  133 us
    reduce_sum x32, other arithmetic, contact(): return (jnp.sum(pushes, 2), -jnp.sum(pushes, 1))  130 us
    scatter-add x32, other arithmetic, visit_block(): totals.at[second_block]  116 us
    scatter-add x32, other arithmetic, visit_block(): totals.at[first_block]  115 us
    all_gather x1, waiting for transfers between devices, shards(): gathered = lax.all_gather(own_spheres, 'dev', axis=0, tiled=True)  101 us
    reduce_sum x32, other arithmetic, contact(): squared = jnp.sum(separation * separation, 0)  66.4 us
    reduce_scatter x1, waiting for transfers between devices, shards(): summed = lax.psum_scatter(interior, 'dev', scatter_dimension=1, tiled=True)  66.2 us
  transfers between devices with their start and end apart: 6, of which 4 were waited for; matrix products, arithmetic and copies ran while one was open for 1% of the time, Pallas kernels for 0%

commit v1 on v0

--- a/solution.py
+++ b/solution.py
@@ -82,7 +82,10 @@
         jnp.float32
     )
     own_spheres = place_blocks(positions, rotations, onehot, offset_table)
-    gathered = lax.all_gather(own_spheres, "dev", axis=0, tiled=True)
+    count_2 = lax.axis_size("dev")
+    shards_2 = jnp.stack([own_spheres for _ in range(count_2)])
+    shards_2 = lax.all_to_all(shards_2, "dev", split_axis=0, concat_axis=0)
+    gathered = jnp.concatenate(shards_2, axis=0)
     spheres = padded(gathered, (("grp", 0),), RIM)
     table_base = group_index * group_blocks - RIM
     first_local = pair_blocks[0] - table_base

time: 1040 us -> 1100 us (1.058)
  waiting for transfers between devices: 172 us -> 209 us
  local copies, waits for them, and re-layouts: 328 us -> 343 us
    all_to_all x0 -> x1, waiting for transfers between devices: none -> 137 us  [shards(): shards_2 = lax.all_to_all(shards_2, 'dev', split_axis=0, concat_axis=0)]
    all_gather x1 -> x0, waiting for transfers between devices: 101 us -> none  [shards(): gathered = lax.all_gather(own_spheres, 'dev', axis=0, tiled=True)]
where the time goes in v1:
time: 1100 us; the launch traced here: 1090 us
  other arithmetic  495 us (45%)
  local copies, waits for them, and re-layouts  343 us (31%)
  waiting for transfers between devices  209 us (19%)
  between operations  14.9 us (1%)
  starting transfers between devices  12.5 us (1%)
    all_to_all x1, waiting for transfers between devices, shards(): shards_2 = lax.all_to_all(shards_2, 'dev', split_axis=0, concat_axis=0)  137 us
    gather x64, local copies, waits for them, and re-layouts, visit_block(): near_pos = spheres[first_block]  133 us
    gather x64, local copies, waits for them, and re-layouts, visit_block(): far_pos = spheres[second_block]  133 us
    reduce_sum x32, other arithmetic, contact(): return (jnp.sum(pushes, 2), -jnp.sum(pushes, 1))  130 us
    scatter-add x32, other arithmetic, visit_block(): totals.at[second_block]  116 us
    scatter-add x32, other arithmetic, visit_block(): totals.at[first_block]  115 us
    reduce_scatter x1, waiting for transfers between devices, shards(): summed = lax.psum_scatter(interior, 'dev', scatter_dimension=1, tiled=True)  67.2 us
    reduce_sum x32, other arithmetic, contact(): squared = jnp.sum(separation * separation, 0)  66.4 us
  transfers between devices with their start and end apart: 6, of which 4 were waited for; matrix products, arithmetic and copies ran while one was open for 1% of the time, Pallas kernels for 0%

profile of v1, /device:TPU:0, one launch (start us, length us, event | category | flops | bytes accessed | tf_op | source)
XLA Modules:
  0.0 1090.5 jit_solution(1485075344479039239)
XLA Ops:
  13.1 9.7 convolution_add_fusion
  28.2 7.3 all-to-all-start
  36.3 137.5 %all-to-all-done = f32[8,512,3,128]{3,1,2,0:T(8,128)} async-done(((f32[8,512,3,128]{3,1,2,0:T(8,128)}), f32[8,512,3,128]{3,1,2,0:T(8,128)}, u32[]{:S(2)}, u32[]{:S(2)}) %all-to-all-start) | async-done | bytes 6291488 | tf_op jit(solution)/shard_map/all_to_all | solution.py:87
  184.0 19.7 %copy.188 = f32[4352,3,128]{2,1,0:T(4,128)} copy(f32[4352,3,128]{2,0,1:T(8,128)S(1)} %pad_maximum_fusion) | data formatting | bytes 13369344 | tf_op jit(solution)/shard_map/while | solution.py:117
  207.3 792.6 %while.12 = (s32[]{:T(128)}, f32[4352,6,2]{1,2,0:T(2,128)}, s32[]{:T(128)}, s32[1024]{0:T(1024)S(1)}, f32[4352,3,128]{2,1,0:T(4,128)}, /*index=5*/s32[1024]{0:T(...) while((s32[]{:T(128)}, f32[4352,6,2]{1,2,0:T(2,128)}, ...), condition=%wide.region_10.11_spmd, body=%wide.region_0.10_spmd.sunk | while | flops 12222438 | bytes 10249395 | solution.py:117
  207.4 4.1 gather_fusion
  232.2 4.1 gather_fusion
  236.3 4.1 gather_fusion.1
  310.5 4.1 gather_fusion.1
  331.1 4.1 gather_fusion
  360.1 4.1 gather_fusion.1
  384.9 4.1 gather_fusion.1
  409.7 4.1 gather_fusion.1
  455.1 4.1 gather_fusion
  459.2 4.1 gather_fusion.1
  508.8 4.1 gather_fusion.1
  533.5 4.1 gather_fusion.1
  632.5 4.1 gather_fusion.1
  682.0 4.1 gather_fusion.1
  756.3 4.1 gather_fusion.1
  900.8 4.1 gather_fusion
  905.0 4.1 gather_fusion.1
  1002.9 4.4 slice.176
  1014.1 67.2 %reduce-scatter.2.cloned.1.call-done = f32[6,1024]{1,0:T(8,128)} async-done(((f32[6,8192]{1,0:T(8,128)}), f32[6,1024]{1,0:T(8,128)}) %reduce-scatter.2.cloned.1.call-update) | async-done | bytes 24592 | tf_op jit(solution)/shard_map/reduce_scatter | solution.py:129
  (1082 shorter events, 754.6 us)
Async XLA Ops:
  7.2 5.7 copy-start.1
  28.2 145.5 %all-to-all-start = ((f32[8,512,3,128]{3,1,2,0:T(8,128)}), f32[8,512,3,128]{3,1,2,0:T(8,128)}, u32[]{:S(2)}, u32[]{:S(2)}) async-start(f32[8,512,3,128]{3,1,2,0:T(8,128)} %stack.8), calls=%async_computation | async-start | bytes 12582912 | tf_op jit(solution)/shard_map/all_to_all | solution.py:87
  35.5 1045.7 %reduce-scatter.2.cloned.1.call-start = ((), (), s32[]{:S(2)}) async-start(), calls=%async_computation.2 | async-start | bytes 294912 | tf_op jit(solution)/shard_map/reduce_scatter | solution.py:129
  36.2 143.5 %copy-start.2 = (s32[2,1024]{1,0:T(2,128)S(1)}, s32[2,1024]{1,0:T(2,128)}, u32[]{:S(2)}) copy-start(s32[2,1024]{1,0:T(2,128)} %param.16) | copy-start | bytes 24580
  177.2 2.6 collective-permute-start
  178.5 5.1 collective-permute-start.1
  1001.0 10.6 collective-permute-start.2
  1010.3 3.1 collective-permute-start.3
  1013.4 0.7 copy-start
Sparse Core Ops, SparseCore 0:
  1014.2 66.9 reduce-scatter.1
